TPU v7x, 512 devices: a whole 4x4x16 slice. The times are simulated.
512 devices in a mesh: mem: 16 (over z), sp: 32 (over x, y, core).
Axes of the slice: x: 4, y: 4, z: 16, core: 2. Of those that a mesh axis runs over, the one named last changes fastest.
Arguments:
- ensemble: bfloat16 [256, 131072], P('mem', 'sp'), may hold values from -6 to 6
- predicted: bfloat16 [256, 65536], P('mem', 'sp'), may hold values from -2 to 2
- observed: float32 [65536], P('sp'), may hold values from -6 to 6
- perturbation: bfloat16 [256, 65536], P('mem', 'sp'), may hold values from -6 to 6
- noise_variance: float32 [512], P('sp'), may hold values from 0.25 to 4
- block_lists: int32 [32, 64], P('sp'), may hold values from 0 to 511, as said below
- localization: int32 [1024, 64], P('sp'), may hold values 0 or 1
Outputs:
- increment: float32 [256, 131072], P('mem', 'sp')
Inputs may be any that keep to these rules, and one draw needn't show every extreme that they name: `block_lists`: row t lists the 64 distinct data blocks used by the bricks of index t of sp, in increasing order; block j is held by index j // 16; a row uses 1 to 3 blocks of each holder, exactly 3 of some holder, and every holder gives 3 blocks to some row.
All inputs are finite; a program needn't handle non-finite values. No bound on the sum of `localization` on one device may be relied on, other than what follows from the above.
Results may differ from a plain program's by a relative error of at most 0.0055.
Values may be sent and summed in bfloat16 or wider, within the bound.
No kernel may reach another device: no remote copies, remote signals or barrier semaphores. Data moves between devices by JAX's collectives and lax.ppermute only.
A program may use at most 64 MiB of HBM per device.

v0:
```python
import jax
import jax.numpy as jnp
from jax import lax
from jax.sharding import PartitionSpec as P

SLOTS = 3
ENSEMBLE_SCALE = 2.0**13
PREDICTED_SCALE = 2.0**14


def per_device(
    ensemble, predicted, observed, perturbation, noise_variance, block_lists, localization
):
    bf16, f16, f32 = (jnp.bfloat16, jnp.float16, jnp.float32)
    mem, sp = (lax.axis_size("mem"), lax.axis_size("sp"))
    local = ensemble.shape[0]
    members = local * mem
    cells = ensemble.shape[1]
    bricks = localization.shape[0]
    brick = cells // bricks
    blocks = noise_variance.shape[0]
    data = predicted.shape[1]
    block = data // blocks
    need = block_lists.shape[1]
    needed = block_lists[0]
    holder = needed // blocks
    before = jnp.sum(needed[None, :] < (holder * blocks)[:, None], axis=1)
    slot = holder * SLOTS + (jnp.arange(need) - before)
    slot_hot = slot[:, None] == jnp.arange(sp * SLOTS)[None, :]
    asked = jnp.sum(jnp.where(slot_hot, (needed % blocks)[:, None], 0), axis=0)
    asked = jnp.pad(asked.reshape(sp, SLOTS), ((0, 0), (0, 128 - SLOTS)))
    wanted = lax.all_to_all(asked, "sp", split_axis=0, concat_axis=0, tiled=True)
    wanted = wanted[:, :SLOTS].reshape(-1)
    slot_pattern = jnp.dot(
        localization.astype(bf16), slot_hot.astype(bf16), preferred_element_type=f32
    ).astype(bf16)
    sent = jnp.concatenate(
        [
            (predicted.astype(f32) * PREDICTED_SCALE).astype(f16),
            (ensemble.astype(f32) * ENSEMBLE_SCALE).astype(f16),
        ],
        axis=1,
    )
    whole = lax.all_gather(sent, "mem", axis=0, tiled=True)
    whole_predicted = whole[:, :data].astype(f32)
    whole_ensemble = whole[:, data:].astype(f32)
    data_mean = jnp.sum(whole_predicted, axis=0) / members
    data_anomalies = (whole_predicted - data_mean).astype(bf16)
    variance = jnp.repeat(noise_variance, block)
    innovation = (
        observed[None, :] + jnp.sqrt(variance) * perturbation.astype(f32) - predicted.astype(f32)
    )
    weighted = (innovation / variance).astype(bf16)
    products = jnp.einsum(
        "njd,mjd->jnm",
        weighted.reshape(local, blocks, block),
        data_anomalies.reshape(members, blocks, block),
        preferred_element_type=f32,
    ).astype(bf16)
    picked = (wanted[:, None] == jnp.arange(blocks)[None, :]).astype(bf16)
    chosen = jnp.einsum("sj,jnm->snm", picked, products, preferred_element_type=f32).astype(bf16)
    chosen = chosen.reshape(sp, SLOTS * local, members)
    got = lax.all_to_all(chosen, "sp", split_axis=0, concat_axis=0, tiled=True)
    got = got.reshape(sp * SLOTS, local, members)
    gains = jnp.einsum("bs,snm->bnm", slot_pattern, got, preferred_element_type=f32).astype(bf16)
    model_mean = jnp.sum(whole_ensemble, axis=0) / members
    model_anomalies = (whole_ensemble - model_mean).astype(bf16)
    increment = jnp.einsum(
        "bnm,mbc->nbc",
        gains,
        model_anomalies.reshape(members, bricks, brick),
        preferred_element_type=f32,
    )
    return increment.reshape(local, cells) / ((members - 1) * (ENSEMBLE_SCALE * PREDICTED_SCALE))


def solution(mesh):
    in_specs = (
        P("mem", "sp"),
        P("mem", "sp"),
        P("sp"),
        P("mem", "sp"),
        P("sp"),
        P("sp", None),
        P("sp", None),
    )
    return jax.shard_map(
        per_device, mesh=mesh, in_specs=in_specs, out_specs=P("mem", "sp"), check_vma=False
    )
```

profile of v0, /device:TPU:1, one launch (start us, length us, event | category | flops | bytes accessed | tf_op | source)
XLA Modules:
  0.0 100.3 jit_solution(8255561236363733523)
XLA Ops:
  0.0 0.7 broadcast_multiply_fusion.2
  0.7 0.8 convert_reduce_fusion.2
  1.5 0.1 select_reduce_fusion
  1.6 0.1 reshape.108
  1.7 0.6 pad.4
  2.3 10.4 %all-to-all-start = ((s32[32,1,128]{2,1,0:T(1,128)}), s32[32,1,128]{2,1,0:T(1,128)S(1)}, u32[]{:S(2)}, u32[]{:S(2)}) async-start(s32[32,1,128]{2,1,0:T(1,128)} %bitcast.3), calls=%async_computation | async-start | bytes 32768 | tf_op jit(solution)/shard_map/all_to_all | solution.py:32
  12.7 0.7 bitcast_sqrt_fusion
  13.4 0.7 broadcast_bitcast_fusion
  14.2 0.9 multiply_convert_fusion
  15.1 0.9 fusion.24
  16.0 0.1 pad_maximum_fusion
  16.1 50.7 %all-gather.1 = f16[256,6144]{1,0:T(8,128)(2,1)S(1)} all-gather(f16[16,6144]{1,0:T(8,128)(2,1)S(1)} %pad_maximum_fusion), channel_id=1, replica_groups=mesh['mem'=16,'sp'=32] {'mem'}, dimensions={0}, use_global_device_ids=true | all-gather | bytes 3342336 | tf_op jit(solution)/shard_map/all_gather | solution.py:44
  66.8 0.2 convert_reduce_fusion.1
  67.0 0.4 convolution_convert_fusion.2
  67.3 0.0 all-to-all-done
  67.4 0.1 eq.33
  67.5 0.4 convolution_convert_fusion
  67.9 1.3 %copy.33 = bf16[96,16,256]{2,1,0:T(8,128)(2,1)} copy(bf16[96,16,256]{2,0,1:T(8,128)(2,1)S(1)} %convolution_convert_fusion) | data formatting | bytes 1572864 | tf_op jit(solution)/shard_map/convert_element_type | solution.py:61
  69.2 13.9 %all-to-all-start.1 = ((bf16[32,48,256]{2,1,0:T(8,128)(2,1)}), bf16[32,48,256]{2,1,0:T(8,128)(2,1)}, u32[]{:S(2)}, u32[]{:S(2)}) async-start(bf16[32,48,256]{2,1,0:T(8,128)(2,1)} %bitcast.54), calls=%async_computation.1 | async-start | bytes 1572864 | tf_op jit(solution)/shard_map/all_to_all | solution.py:63
  83.1 0.3 convert_reduce_fusion
  83.4 14.0 %all-to-all-done.1 = bf16[32,48,256]{2,1,0:T(8,128)(2,1)} async-done(((bf16[32,48,256]{2,1,0:T(8,128)(2,1)}), bf16[32,48,256]{2,1,0:T(8,128)(2,1)}, u32[]{:S(2)}, u32[]{:S(2)}) %all-to-all-start.1) | async-done | bytes 786464 | tf_op jit(solution)/shard_map/all_to_all | solution.py:63
  97.4 1.6 %convolution_convert_fusion.1 = bf16[32,16,256]{2,0,1:T(8,128)(2,1)S(1)} fusion(bf16[96,16,256]{2,1,0:T(8,128)(2,1)} %bitcast.8, s32[64]{0:T(128)S(1)} %subtract_add_fusion, s32[32,64]{1,0:T(8,128)S(1)} %copy-done), kind=kOutput, calls=%fused_computation.11 | convolution fusion | flops 25701376 | bytes 1057024 | tf_op jit(solution)/shard_map/bs,snm->bnm/dot_general | solution.py:65
  99.0 0.6 fusion.9
  99.5 0.7 copy.65
  (5 shorter events, 0.0 us)
Async XLA Ops:
  2.3 65.0 %all-to-all-start = ((s32[32,1,128]{2,1,0:T(1,128)}), s32[32,1,128]{2,1,0:T(1,128)S(1)}, u32[]{:S(2)}, u32[]{:S(2)}) async-start(s32[32,1,128]{2,1,0:T(1,128)} %bitcast.3), calls=%async_computation | async-start | bytes 32768 | tf_op jit(solution)/shard_map/all_to_all | solution.py:32
  67.3 30.0 %copy-start = (s32[32,64]{1,0:T(8,128)S(1)}, s32[32,64]{1,0:T(8,128)}, u32[]{:S(2)}) copy-start(s32[32,64]{1,0:T(8,128)} %param.13) | copy-start | bytes 24580
  69.2 28.2 %all-to-all-start.1 = ((bf16[32,48,256]{2,1,0:T(8,128)(2,1)}), bf16[32,48,256]{2,1,0:T(8,128)(2,1)}, u32[]{:S(2)}, u32[]{:S(2)}) async-start(bf16[32,48,256]{2,1,0:T(8,128)(2,1)} %bitcast.54), calls=%async_computation.1 | async-start | bytes 1572864 | tf_op jit(solution)/shard_map/all_to_all | solution.py:63
where the time goes:
time: 101 us; the launch traced here: 100 us
  blocking collectives  50.7 us (50%)
  starting transfers between devices  24.2 us (24%)
  waiting for transfers between devices  14 us (14%)
  local copies, waits for them, and re-layouts  4.36 us (4%)
  other arithmetic  4 us (4%)
  matrix products  2.93 us (3%)
    all_gather x1, blocking collectives, per_device(): whole = lax.all_gather(sent, 'mem', axis=0, tiled=True)  50.7 us
    all_to_all x1, waiting for transfers between devices, per_device(): got = lax.all_to_all(chosen, 'sp', split_axis=0, concat_axis=0, tiled=True)  14 us
    all_to_all x1, starting transfers between devices, per_device(): got = lax.all_to_all(chosen, 'sp', split_axis=0, concat_axis=0, tiled=True)  13.9 us
    all_to_all x1, starting transfers between devices, per_device(): lax.all_to_all(asked, 'sp', split_axis=0, concat_axis=0, tiled=True)  10.4 us
  transfers between devices with their start and end apart: 2, of which 1 were waited for; matrix products, arithmetic and copies ran while one was open for 4% of the time, Pallas kernels for 0%

commit v1 on v0

--- a/solution.py
+++ b/solution.py
@@ -41,7 +41,9 @@
         ],
         axis=1,
     )
-    whole = lax.all_gather(sent, "mem", axis=0, tiled=True)
+    whole = jnp.concatenate(
+        lax.all_to_all(jnp.stack([sent] * lax.axis_size("mem")), "mem", 0, 0), axis=0
+    )
     whole_predicted = whole[:, :data].astype(f32)
     whole_ensemble = whole[:, data:].astype(f32)
     data_mean = jnp.sum(whole_predicted, axis=0) / members

time: 101 us -> 200 us (1.98)
  waiting for transfers between devices: 14 us -> 150 us
  blocking collectives: 50.7 us -> 0 us
  starting transfers between devices: 24.2 us -> 31.1 us
  local copies, waits for them, and re-layouts: 4.36 us -> 9.64 us
    all_to_all x0 -> x1, waiting for transfers between devices: none -> 137 us  [per_device(): lax.all_to_all(jnp.stack([sent] * lax.axis_size('mem')), 'mem', 0, 0)]
    all_gather x1 -> x0, blocking collectives: 50.7 us -> none  [per_device(): whole = lax.all_gather(sent, 'mem', axis=0, tiled=True)]
    all_to_all x0 -> x1, starting transfers between devices: none -> 13 us  [per_device(): lax.all_to_all(jnp.stack([sent] * lax.axis_size('mem')), 'mem', 0, 0)]
    all_to_all x1, starting transfers between devices: 13.9 us -> 7.74 us  [per_device(): got = lax.all_to_all(chosen, 'sp', split_axis=0, concat_axis=0, tiled=True)]
    all_to_all x1, waiting for transfers between devices: 14 us -> 9.3 us  [per_device(): got = lax.all_to_all(chosen, 'sp', split_axis=0, concat_axis=0, tiled=True)]
    all_to_all x1, waiting for transfers between devices: 0.01 us -> 3.59 us  [per_device(): lax.all_to_all(asked, 'sp', split_axis=0, concat_axis=0, tiled=True)]
    convert_element_type x0 -> x1, local copies, waits for them, and re-layouts: none -> 3.28 us  [per_device(): model_anomalies = (whole_ensemble - model_mean).astype(bf16)]
    another operation x0 -> x1, local copies, waits for them, and re-layouts: none -> 2.03 us  [per_device(): jnp.stack([sent] * lax.axis_size('mem'))]
  transfers between devices with their start and end apart: 2 -> 3, of which waited for: 1 -> 3; matrix products, arithmetic and copies ran while one was open for 4% -> 4% of each run, Pallas kernels for 0% -> 0%
where the time goes in v1:
time: 200 us; the launch traced here: 199 us
  waiting for transfers between devices  150 us (75%)
  starting transfers between devices  31.1 us (16%)
  local copies, waits for them, and re-layouts  9.64 us (5%)
  other arithmetic  5.79 us (3%)
  matrix products  3.04 us (2%)
    all_to_all x1, waiting for transfers between devices, per_device(): lax.all_to_all(jnp.stack([sent] * lax.axis_size('mem')), 'mem', 0, 0)  137 us
    all_to_all x1, starting transfers between devices, per_device(): lax.all_to_all(jnp.stack([sent] * lax.axis_size('mem')), 'mem', 0, 0)  13 us
    all_to_all x1, starting transfers between devices, per_device(): lax.all_to_all(asked, 'sp', split_axis=0, concat_axis=0, tiled=True)  10.4 us
    all_to_all x1, waiting for transfers between devices, per_device(): got = lax.all_to_all(chosen, 'sp', split_axis=0, concat_axis=0, tiled=True)  9.3 us
    all_to_all x1, starting transfers between devices, per_device(): got = lax.all_to_all(chosen, 'sp', split_axis=0, concat_axis=0, tiled=True)  7.74 us
  transfers between devices with their start and end apart: 3, of which 3 were waited for; matrix products, arithmetic and copies ran while one was open for 4% of the time, Pallas kernels for 0%

profile of v1, /device:TPU:1, one launch (start us, length us, event | category | flops | bytes accessed | tf_op | source)
XLA Modules:
  0.0 199.3 jit_solution(4354237936454875738)
XLA Ops:
  0.0 0.7 broadcast_multiply_fusion.2
  0.7 0.8 convert_reduce_fusion.2
  1.7 0.6 pad.4
  2.3 10.4 %all-to-all-start.1 = ((s32[32,1,128]{2,1,0:T(1,128)}), s32[32,1,128]{2,1,0:T(1,128)S(1)}, u32[]{:S(2)}, u32[]{:S(2)}) async-start(s32[32,1,128]{2,1,0:T(1,128)} %bitcast.5), calls=%async_computation.1 | async-start | bytes 32768 | tf_op jit(solution)/shard_map/all_to_all | solution.py:32
  12.7 0.7 bitcast_sqrt_fusion
  13.4 0.7 broadcast_bitcast_fusion
  14.2 0.9 multiply_convert_fusion
  15.1 0.9 fusion.15
  16.1 3.6 %all-to-all-done.1 = s32[32,1,128]{2,1,0:T(1,128)S(1)} async-done(((s32[32,1,128]{2,1,0:T(1,128)}), s32[32,1,128]{2,1,0:T(1,128)S(1)}, u32[]{:S(2)}, u32[]{:S(2)}) %all-to-all-start.1) | async-done | bytes 16416 | tf_op jit(solution)/shard_map/all_to_all | solution.py:32
  19.7 2.0 %stack.2 = f16[16,16,6144]{2,1,0:T(8,128)(2,1)} broadcast(f16[16,6144]{1,0:T(8,128)(2,1)S(1)} %pad_maximum_fusion), dimensions={1,2} | broadcast | bytes 3342336 | tf_op jit(solution)/shard_map/stack | solution.py:45
  21.7 13.0 %all-to-all-start = ((f16[16,16,6144]{2,1,0:T(8,128)(2,1)}), f16[16,16,6144]{2,1,0:T(8,128)(2,1)S(1)}, u32[]{:S(2)}, u32[]{:S(2)}) async-start(f16[16,16,6144]{2,1,0:T(8,128)(2,1)} %stack.2), calls=%async_computation | async-start | bytes 6291456 | tf_op jit(solution)/shard_map/all_to_all | solution.py:45
  34.9 136.7 %all-to-all-done = f16[16,16,6144]{2,1,0:T(8,128)(2,1)S(1)} async-done(((f16[16,16,6144]{2,1,0:T(8,128)(2,1)}), f16[16,16,6144]{2,1,0:T(8,128)(2,1)S(1)}, u32[]{:S(2)}, u32[]{:S(2)}) %all-to-all-start) | async-done | bytes 3145760 | tf_op jit(solution)/shard_map/all_to_all | solution.py:45
  171.6 0.2 convert_reduce_fusion.1
  171.7 0.3 convert_reduce_fusion
  172.1 0.4 convolution_convert_fusion.2
  172.4 0.4 convolution_convert_fusion
  172.9 1.3 copy.44
  174.2 7.7 %all-to-all-start.2 = ((bf16[32,48,256]{2,1,0:T(8,128)(2,1)}), bf16[32,48,256]{2,1,0:T(8,128)(2,1)}, u32[]{:S(2)}, u32[]{:S(2)}) async-start(bf16[32,48,256]{2,1,0:T(8,128)(2,1)} %bitcast.51), calls=%async_computation.2 | async-start | bytes 1572864 | tf_op jit(solution)/shard_map/all_to_all | solution.py:65
  181.9 1.8 fusion
  183.7 3.3 %copy.39 = bf16[256,4096]{0,1:T(8,128)(2,1)S(1)} copy(bf16[256,4096]{1,0:T(8,128)(2,1)} %fusion) | data formatting | bytes 4194304 | tf_op jit(solution)/shard_map/convert_element_type | solution.py:69
  187.0 9.3 %all-to-all-done.2 = bf16[32,48,256]{2,1,0:T(8,128)(2,1)} async-done(((bf16[32,48,256]{2,1,0:T(8,128)(2,1)}), bf16[32,48,256]{2,1,0:T(8,128)(2,1)}, u32[]{:S(2)}, u32[]{:S(2)}) %all-to-all-start.2) | async-done | bytes 786464 | tf_op jit(solution)/shard_map/all_to_all | solution.py:65
  196.3 1.6 convolution_convert_fusion.1
  197.9 0.7 fusion.2
  198.6 0.7 copy.68
  (9 shorter events, 0.4 us)
Async XLA Ops:
  2.3 17.3 %all-to-all-start.1 = ((s32[32,1,128]{2,1,0:T(1,128)}), s32[32,1,128]{2,1,0:T(1,128)S(1)}, u32[]{:S(2)}, u32[]{:S(2)}) async-start(s32[32,1,128]{2,1,0:T(1,128)} %bitcast.5), calls=%async_computation.1 | async-start | bytes 32768 | tf_op jit(solution)/shard_map/all_to_all | solution.py:32
  21.7 149.8 %all-to-all-start = ((f16[16,16,6144]{2,1,0:T(8,128)(2,1)}), f16[16,16,6144]{2,1,0:T(8,128)(2,1)S(1)}, u32[]{:S(2)}, u32[]{:S(2)}) async-start(f16[16,16,6144]{2,1,0:T(8,128)(2,1)} %stack.2), calls=%async_computation | async-start | bytes 6291456 | tf_op jit(solution)/shard_map/all_to_all | solution.py:45
  174.2 22.1 %all-to-all-start.2 = ((bf16[32,48,256]{2,1,0:T(8,128)(2,1)}), bf16[32,48,256]{2,1,0:T(8,128)(2,1)}, u32[]{:S(2)}, u32[]{:S(2)}) async-start(bf16[32,48,256]{2,1,0:T(8,128)(2,1)} %bitcast.51), calls=%async_computation.2 | async-start | bytes 1572864 | tf_op jit(solution)/shard_map/all_to_all | solution.py:65
  183.7 12.6 %copy-start = (s32[32,64]{1,0:T(8,128)S(1)}, s32[32,64]{1,0:T(8,128)}, u32[]{:S(2)}) copy-start(s32[32,64]{1,0:T(8,128)} %param.13) | copy-start | bytes 24580
